TPU v7x, 256 devices: a whole 4x4x8 slice. The times are simulated.
256 devices in a mesh: det: 64 (over x, z, core), head: 4 (over y).
Axes of the slice: x: 4, y: 4, z: 8, core: 2. Of those that a mesh axis runs over, the one named last changes fastest.
Arguments:
- elements: bfloat16 [32768, 1024], P('det'), may hold values from -6 to 6
- element_types: int32 [32768], P('det'), may hold values from 0 to 1, as said below
- handover_counts: int32 [64, 64], replicated, may hold values from 0 to 16, as said below
- block_lists: int32 [256, 16], P('det'), may hold values from 0 to 255, as said below
- w_first: bfloat16 [2, 1024, 2048], P(None, None, 'head'), may hold values from -0.1875 to 0.1875
- w_second: bfloat16 [2, 2048, 1024], P(None, 'head'), may hold values from -0.125 to 0.125
- w_query: bfloat16 [1024, 1024], P(None, 'head'), may hold values from -3 to 3
- key_value_weight: bfloat16 [1024, 2, 256], P(None, None, 'head'), may hold values from -0.1875 to 0.1875
- attention_cotangent: bfloat16 [32768, 1024], P('det', 'head'), may hold values from -6 to 6
Outputs:
- attended: bfloat16 [32768, 1024], P('det', 'head')
- x_grad: bfloat16 [32768, 1024], P('det', 'head')
Inputs may be any that keep to these rules, and one draw needn't show every extreme that they name: `element_types`: of the 512 elements of each device of det, exactly 256 are of each type. `handover_counts`: row d, column e counts the elements that device d of det hands to device e; every row and every column sums to 512; some entries equal 16. `block_lists`: key block k is held by device k // 4 of det; the 16 entries of a query block may repeat; the lists of the 4 query blocks of one device together name exactly 1 block, counted with repeats, held by each device of det.
All inputs are finite; a program needn't handle non-finite values.
Results may differ from a plain program's by a relative error of at most 0.024.
The roundings to bfloat16 on the way count: a program that leaves them out, or rounds other values in their place, can miss the bound.
Values may be sent and summed in bfloat16 or wider, within the bound.
A program may use at most 64 MiB of HBM per device.

v0:
```python
import jax
import jax.numpy as jnp
from jax import lax
from jax.sharding import PartitionSpec as P

HEAD_SIZE = 64
BLOCK_ROWS = 128
LISTED_COUNT = 16
GROUP_HEADS = 4


def exclusive(counts, reduce_axis):
    return jnp.cumsum(counts, axis=reduce_axis, dtype=jnp.int32) - counts


def pack_rows(source_rows, starts, amounts, capacity):
    slot_ids = jnp.arange(capacity, dtype=jnp.int32)
    row_index = jnp.clip(starts[:, None] + slot_ids[None, :], 0, source_rows.shape[0] - 1)
    usable = slot_ids[None, :] < amounts[:, None]
    picked = source_rows[row_index.reshape(-1)].reshape(
        amounts.shape[0], capacity, source_rows.shape[1]
    )
    return jnp.where(usable[:, :, None], picked, jnp.zeros_like(picked))


def unpack_rows(received, starts, amounts, total_rows):
    peer_count, capacity = (received.shape[0], received.shape[1])
    within = jnp.arange(total_rows, dtype=jnp.int32)
    end_rows = starts + amounts
    peer_ids = jnp.sum(
        (end_rows[None, :] <= within[:, None]).astype(jnp.int32), axis=1, dtype=jnp.int32
    )
    slot_ids = within - starts[peer_ids]
    flattened = received.reshape(peer_count * capacity, received.shape[2])
    return flattened[peer_ids * capacity + slot_ids]


def attend(query_block_one, cotangent_block, key_block_rows, value_block_rows):
    score_scaling = HEAD_SIZE ** (-0.5)
    score_matrix = (
        jnp.einsum(
            "oenl,iel->enoi", query_block_one, key_block_rows, preferred_element_type=jnp.float32
        )
        * score_scaling
    )
    row_max = jnp.max(score_matrix, axis=-1, keepdims=True)
    exp_scores = jnp.exp(score_matrix - row_max)
    probability = exp_scores / jnp.sum(exp_scores, axis=-1, keepdims=True)
    probability_bfloat = probability.astype(jnp.bfloat16)
    attended = jnp.einsum(
        "vnys,svx->yvnx", probability_bfloat, value_block_rows, preferred_element_type=jnp.float32
    ).astype(jnp.bfloat16)
    probability_gradient = jnp.einsum(
        "oenl,iel->enoi", cotangent_block, value_block_rows, preferred_element_type=jnp.float32
    )
    row_delta = jnp.sum(probability * probability_gradient, axis=-1, keepdims=True)
    score_gradient = (probability * (probability_gradient - row_delta)).astype(jnp.bfloat16)
    query_gradient = (
        jnp.einsum(
            "vnys,svx->yvnx", score_gradient, key_block_rows, preferred_element_type=jnp.float32
        )
        * score_scaling
    ).astype(jnp.bfloat16)
    key_gradient = (
        jnp.einsum(
            "njtw,tnjs->wns", score_gradient, query_block_one, preferred_element_type=jnp.float32
        )
        * score_scaling
    )
    value_gradient = jnp.einsum(
        "njtw,tnjs->wns", probability_bfloat, cotangent_block, preferred_element_type=jnp.float32
    )
    return (attended, query_gradient, key_gradient, value_gradient)


def shards(
    elements,
    element_types,
    handover_counts,
    block_lists,
    w_first,
    w_second,
    w_query,
    key_value_weight,
    attention_cotangent,
):
    peer_count = lax.axis_size("det")
    my_index = lax.axis_index("det")
    row_count = elements.shape[0]
    model_width = elements.shape[1]
    capacity = 2 * row_count // peer_count
    starts = exclusive(handover_counts, 1)
    offsets = exclusive(handover_counts, 0)
    send_starts = lax.dynamic_index_in_dim(starts, my_index, 0, keepdims=False)
    send_counts = lax.dynamic_index_in_dim(handover_counts, my_index, 0, keepdims=False)
    recv_starts = lax.dynamic_index_in_dim(offsets, my_index, 1, keepdims=False)
    recv_counts = lax.dynamic_index_in_dim(handover_counts, my_index, 1, keepdims=False)
    type_count = w_first.shape[0]
    per_type = row_count // type_count
    type_order = jnp.argsort(element_types, stable=True)
    back_order = (
        jnp.zeros_like(type_order).at[type_order].set(jnp.arange(row_count, dtype=jnp.int32))
    )
    sorted_rows = elements[type_order].reshape(type_count, per_type, model_width)
    preact = jnp.einsum("trd,tdh->trh", sorted_rows, w_first, preferred_element_type=jnp.float32)
    hidden = jax.nn.gelu(preact).astype(jnp.bfloat16)
    sorted_mlp = jnp.einsum("trh,thd->trd", hidden, w_second, preferred_element_type=jnp.float32)
    partial_mlp = sorted_mlp.reshape(row_count, model_width)[back_order]
    mlp_sum = lax.psum(partial_mlp, "head")
    mixed = (elements.astype(jnp.float32) + mlp_sum).astype(jnp.bfloat16)
    outbound = pack_rows(mixed, send_starts, send_counts, capacity)
    inbound = lax.all_to_all(outbound, "det", split_axis=0, concat_axis=0, tiled=True)
    moved = unpack_rows(inbound, recv_starts, recv_counts, row_count)
    kv_width = key_value_weight.shape[2]
    key_value_flat = key_value_weight.reshape(model_width, 2 * kv_width)
    query_rows_all = jnp.dot(moved, w_query, preferred_element_type=jnp.float32).astype(
        jnp.bfloat16
    )
    key_value_pairs = jnp.dot(moved, key_value_flat, preferred_element_type=jnp.float32).astype(
        jnp.bfloat16
    )
    blocks_dev = row_count // BLOCK_ROWS
    slot_count = blocks_dev * LISTED_COUNT
    per_pair = slot_count // peer_count
    flat_list = block_lists.reshape(slot_count)
    owners = flat_list // blocks_dev
    local_ids = flat_list % blocks_dev
    slot_order = jnp.arange(slot_count, dtype=jnp.int32)
    earlier = (owners[:, None] == owners[None, :]) & (slot_order[None, :] < slot_order[:, None])
    slot_rank = jnp.sum(earlier.astype(jnp.int32), axis=1, dtype=jnp.int32)
    position = owners * per_pair + slot_rank
    requests = (
        jnp.zeros((slot_count,), jnp.int32)
        .at[position]
        .set(local_ids)
        .reshape(peer_count, per_pair)
    )
    wanted = lax.all_to_all(requests, "det", split_axis=0, concat_axis=0, tiled=True)
    all_keys = lax.all_gather(key_value_pairs, "det", axis=0, tiled=True)
    listed = all_keys.reshape(-1, BLOCK_ROWS, 2 * kv_width)[flat_list]
    listed = listed.reshape(blocks_dev, LISTED_COUNT * BLOCK_ROWS, 2 * kv_width)
    kv_heads = kv_width // HEAD_SIZE
    query_block_list = query_rows_all.reshape(
        blocks_dev, BLOCK_ROWS, kv_heads, GROUP_HEADS, HEAD_SIZE
    )
    cotangent_blocks = attention_cotangent.reshape(
        blocks_dev, BLOCK_ROWS, kv_heads, GROUP_HEADS, HEAD_SIZE
    )

    def one_block(inputs):
        query_block_one, cotangent_block, key_value_rows = inputs
        key_block_rows = key_value_rows[:, :kv_width].reshape(
            LISTED_COUNT * BLOCK_ROWS, kv_heads, HEAD_SIZE
        )
        value_block_rows = key_value_rows[:, kv_width:].reshape(
            LISTED_COUNT * BLOCK_ROWS, kv_heads, HEAD_SIZE
        )
        return attend(query_block_one, cotangent_block, key_block_rows, value_block_rows)

    attended, query_gradient, key_gradient, value_gradient = lax.map(
        one_block, (query_block_list, cotangent_blocks, listed)
    )
    slot_gradients = jnp.concatenate(
        [
            key_gradient.reshape(blocks_dev, LISTED_COUNT * BLOCK_ROWS, kv_width),
            value_gradient.reshape(blocks_dev, LISTED_COUNT * BLOCK_ROWS, kv_width),
        ],
        axis=2,
    )
    slot_gradients = slot_gradients.reshape(slot_count, BLOCK_ROWS, 2 * kv_width).astype(
        jnp.bfloat16
    )
    returned = (
        jnp.zeros_like(slot_gradients)
        .at[position]
        .set(slot_gradients)
        .reshape(peer_count, per_pair, BLOCK_ROWS, 2 * kv_width)
    )
    collected = lax.all_to_all(returned, "det", split_axis=0, concat_axis=0, tiled=True)
    collected = collected.reshape(slot_count, BLOCK_ROWS, 2 * kv_width).astype(jnp.float32)
    key_gradient_total = (
        jnp.zeros((blocks_dev, BLOCK_ROWS, 2 * kv_width), jnp.float32)
        .at[wanted.reshape(-1)]
        .add(collected)
    )
    key_bfloat = key_gradient_total.reshape(row_count, 2 * kv_width).astype(jnp.bfloat16)
    contract = (((1,), (1,)), ((), ()))
    partial_back = lax.dot_general(
        query_gradient.reshape(row_count, -1), w_query, contract, preferred_element_type=jnp.float32
    )
    partial_back = partial_back + lax.dot_general(
        key_bfloat, key_value_flat, contract, preferred_element_type=jnp.float32
    )
    back_sum = lax.psum(partial_back, "head").astype(jnp.bfloat16)
    outbound_back = pack_rows(back_sum, recv_starts, recv_counts, capacity)
    inbound_back = lax.all_to_all(outbound_back, "det", split_axis=0, concat_axis=0, tiled=True)
    upstream = unpack_rows(inbound_back, send_starts, send_counts, row_count)
    sorted_up = upstream[type_order].reshape(type_count, per_type, model_width)
    hidden_grad = jnp.einsum(
        "trd,thd->trh", sorted_up, w_second, preferred_element_type=jnp.float32
    )
    preact_grad = jax.vjp(jax.nn.gelu, preact)[1](hidden_grad)[0].astype(jnp.bfloat16)
    sorted_input = jnp.einsum(
        "trh,tdh->trd", preact_grad, w_first, preferred_element_type=jnp.float32
    )
    input_part = sorted_input.reshape(row_count, model_width)[back_order]
    input_share = lax.psum_scatter(input_part, "head", scatter_dimension=1, tiled=True)
    share_width = input_share.shape[1]
    own_upstream = lax.dynamic_slice_in_dim(
        upstream, lax.axis_index("head") * share_width, share_width, 1
    )
    x_grad = (own_upstream.astype(jnp.float32) + input_share).astype(jnp.bfloat16)
    return (attended.reshape(row_count, -1), x_grad)


def solution(mesh):
    return jax.shard_map(
        shards,
        mesh=mesh,
        in_specs=(
            P("det", None),
            P("det"),
            P(),
            P("det", None),
            P(None, None, "head"),
            P(None, "head", None),
            P(None, "head"),
            P(None, None, "head"),
            P("det", "head"),
        ),
        out_specs=(P("det", "head"), P("det", "head")),
        check_vma=False,
    )
```

profile of v0, /device:TPU:1, one launch (start us, length us, event | category | flops | bytes accessed | tf_op | source)
XLA Modules:
  0.0 602.9 jit_solution(14626544373594868727)
XLA Ops:
  7.2 4.6 sort.17
  11.8 2.4 scatter_custom_fusion
  14.3 4.1 gather_fusion
  18.4 2.3 fusion.99
  20.8 2.2 fusion.52
  22.9 5.3 gather_fusion.1
  29.4 66.3 %all-reduce.3.cloned.1.call-done = f32[512,1024]{1,0:T(8,128)} async-done(((f32[512,1024]{1,0:T(8,128)}), f32[512,1024]{1,0:T(8,128)}) %all-reduce.3.cloned.1.call-update) | async-done | bytes 2097168 | tf_op jit(solution)/shard_map/psum | solution.py:109
  95.8 2.2 add_convert_fusion
  98.0 5.4 gather_fusion.2
  103.4 3.2 broadcast_select_fusion.1
  106.6 11.0 %all-to-all-start = ((bf16[64,16,1024]{2,1,0:T(8,128)(2,1)}), bf16[64,16,1024]{2,1,0:T(8,128)(2,1)}, u32[]{:S(2)}, u32[]{:S(2)}) async-start(bf16[64,16,1024]{2,1,0:T(8,128)(2,1)} %broadcast_select_fusion.1), calls=%async_computation | async-start | bytes 4194304 | tf_op jit(solution)/shard_map/all_to_all | solution.py:112
  123.6 4.3 compare_select_fusion.12
  128.2 4.3 compare_select_fusion.6
  132.9 35.3 %select_select_fusion.1 = s32[512]{0:T(512)S(1)} fusion(pred[512]{0:T(512)(128)(4,1)S(1)} %get-tuple-element.224, pred[512]{0:T(512)(128)(4,1)S(1)} %get-tuple-element.223, pred[512]{0:T(512)(128)(4,1)S(1)} %get-tuple-element.222, pred[512]{0:T(512)(128)(4,1)S(1)} %get-tuple-element.221, pred[512]{0:T(512)(128)(4,1)S(1)} %get-tuple-element.220, ...), kind=kLoop, calls=%fused_computation.250 | loop fusion | flops 29184 | bytes 33508 | tf_op jit(solution)/shard_map/gather | solution.py:33
  168.3 35.6 %select_select_fusion = s32[512]{0:T(512)S(1)} fusion(pred[512]{0:T(512)(128)(4,1)S(1)} %get-tuple-element.167, pred[512]{0:T(512)(128)(4,1)S(1)} %get-tuple-element.166, pred[512]{0:T(512)(128)(4,1)S(1)} %get-tuple-element.165, pred[512]{0:T(512)(128)(4,1)S(1)} %get-tuple-element.164, pred[512]{0:T(512)(128)(4,1)S(1)} %get-tuple-element.163, ...), kind=kLoop, calls=%fused_computation.249 | loop fusion | flops 29184 | bytes 33508 | tf_op jit(solution)/shard_map/gather | solution.py:33
  204.0 4.6 gather_fusion.3
  210.1 10.0 %scatter_custom_fusion.1 = s32[64]{0:T(128)S(1)} fusion(s32[64]{0:T(128)S(1)} %get-tuple-element.385, s32[64]{0:T(128)S(1)} %get-tuple-element.383, s32[]{:T(128)} %constant.56.clone.1), kind=kCustom, calls=%fused_computation.271 | custom fusion | bytes 260 | tf_op jit(solution)/shard_map/scatter | solution.py:135
  220.8 10.3 %all-to-all-start.1 = ((s32[64,1,1]{2,1,0:T(1,128)}), s32[64,1,1]{2,1,0:T(1,128)S(1)}, u32[]{:S(2)}, u32[]{:S(2)}) async-start(s32[64,1,1]{2,1,0:T(1,128)} %copy.91), calls=%async_computation.1 | async-start | bytes 65536 | tf_op jit(solution)/shard_map/all_to_all | solution.py:138
  231.2 2.1 reshape.1340
  233.3 1.9 copy.88
  235.2 1.5 convolution_convert_fusion
  237.2 55.5 %all-gather.2.cloned.1.call-done = bf16[32768,128]{1,0:T(8,128)(2,1)} async-done(((bf16[512,128]{1,0:T(8,128)(2,1)}), bf16[32768,128]{1,0:T(8,128)(2,1)}) %all-gather.2.cloned.1.call-update) | async-done | bytes 8388624 | tf_op jit(solution)/shard_map/all_gather | solution.py:139
  292.7 5.6 gather_fusion.4
  298.3 41.0 %while.16 = (s32[]{:T(128)}, bf16[4,128,1,4,64]{1,4,3,2,0:T(8,128)(2,1)}, bf16[4,128,1,4,64]{1,4,3,2,0:T(8,128)(2,1)}, bf16[4,2048,1,64]{1,3,2,0:T(8,128)(2,1)},...) while((s32[]{:T(128)}, ...), condition=%wide.region_10.11_spmd, body=%wide.region_6.10_spmd.sunk | while | flops 830700032 | bytes 62289140 | solution.py:160
  302.6 1.3 fusion.137
  303.9 1.1 fusion.138
  305.9 1.1 fusion.139
  307.0 1.6 fusion.136
  312.9 1.3 fusion.137
  314.2 1.1 fusion.138
  316.2 1.1 fusion.139
  317.3 1.6 fusion.136
  323.2 1.3 fusion.137
  326.4 1.1 fusion.139
  327.6 1.6 fusion.136
  333.4 1.3 fusion.137
  336.7 1.1 fusion.139
  337.8 1.6 fusion.136
  339.4 2.0 copy.93
  341.4 1.5 concatenate.10
  342.9 2.0 copy.92
  345.0 1.5 concatenate.9
  346.5 3.1 pad_maximum_fusion
  349.5 4.2 copy.94
  353.7 1.9 broadcast_in_dim.43
  355.6 10.0 %scatter_fusion = bf16[64,128,128]{2,1,0:T(8,128)(2,1)} fusion(bf16[64,128,128]{2,1,0:T(8,128)(2,1)} %broadcast_in_dim.43, s32[64]{0:T(128)S(1)} %get-tuple-element.385, bf16[64,128,128]{2,1,0:T(8,128)(2,1)} %copy.94), kind=kCustom, calls=%fused_computation.11 | custom fusion | bytes 6291712 | tf_op jit(solution)/shard_map/scatter | solution.py:176
  365.6 6.0 %all-to-all-start.2 = ((bf16[64,1,128,128]{3,2,1,0:T(8,128)(2,1)}), bf16[64,1,128,128]{3,2,1,0:T(8,128)(2,1)}, u32[]{:S(2)}, u32[]{:S(2)}) async-start(bf16[64,1,128,128]{3,2,1,0:T(8,128)(2,1)} %bitcast.379), calls=%async_computation.2 | async-start | bytes 4194304 | tf_op jit(solution)/shard_map/all_to_all | solution.py:179
  371.9 1.2 reduce.62
  373.3 49.4 %all-to-all-done.2 = bf16[64,1,128,128]{3,2,1,0:T(8,128)(2,1)} async-done(((bf16[64,1,128,128]{3,2,1,0:T(8,128)(2,1)}), bf16[64,1,128,128]{3,2,1,0:T(8,128)(2,1)}, u32[]{:S(2)}, u32[]{:S(2)}) %all-to-all-start.2) | async-done | bytes 2097184 | tf_op jit(solution)/shard_map/all_to_all | solution.py:179
  422.7 4.0 bitcast_convert_fusion
  426.8 8.8 %scatter_fusion.1 = f32[4,128,128]{2,1,0:T(8,128)S(1)} fusion(f32[4,128,128]{2,1,0:T(8,128)S(1)} %broadcast_in_dim.42, s32[64]{0:T(128)S(1)} %fusion.73, f32[64,128,128]{2,1,0:T(8,128)} %bitcast_convert_fusion), kind=kCustom, calls=%fused_computation.12 | custom fusion | flops 1048576 | bytes 12583168 | tf_op jit(solution)/shard_map/scatter-add | solution.py:184
  436.6 1.8 convolution_add_fusion
  438.5 42.7 %all-reduce.4 = bf16[512,1024]{1,0:T(8,128)(2,1)S(1)} all-reduce(f32[512,1024]{1,0:T(8,128)} %convolution_add_fusion), channel_id=1, replica_groups=mesh['det'=64,'head'=4] {'head'}, use_global_device_ids=true, to_apply=%region_15.16 | all-reduce | flops 524288 | bytes 3145728 | tf_op jit(solution)/shard_map/psum | solution.py:194
  481.2 5.4 gather_fusion.5
  486.6 3.2 broadcast_select_fusion
  489.8 8.1 %all-to-all-start.3 = ((bf16[64,16,1024]{2,1,0:T(8,128)(2,1)}), bf16[64,16,1024]{2,1,0:T(8,128)(2,1)}, u32[]{:S(2)}, u32[]{:S(2)}) async-start(bf16[64,16,1024]{2,1,0:T(8,128)(2,1)} %broadcast_select_fusion), calls=%async_computation.3 | async-start | bytes 4194304 | tf_op jit(solution)/shard_map/all_to_all | solution.py:196
  497.9 51.1 %all-to-all-done.3 = bf16[64,16,1024]{2,1,0:T(8,128)(2,1)} async-done(((bf16[64,16,1024]{2,1,0:T(8,128)(2,1)}), bf16[64,16,1024]{2,1,0:T(8,128)(2,1)}, u32[]{:S(2)}, u32[]{:S(2)}) %all-to-all-start.3) | async-done | bytes 2097184 | tf_op jit(solution)/shard_map/all_to_all | solution.py:196
  548.9 4.6 gather_fusion.6
  553.5 2.8 gather_fusion.7
  556.3 5.3 fusion.53
  561.7 5.2 gather_fusion.8
  568.9 2.2 reshape.1341
  571.1 23.1 %reduce-scatter.2.cloned.1.call-done = f32[512,256]{1,0:T(8,128)} async-done(((f32[512,1024]{1,0:T(8,128)}), f32[512,256]{1,0:T(8,128)}) %reduce-scatter.2.cloned.1.call-update) | async-done | bytes 524304 | tf_op jit(solution)/shard_map/reduce_scatter | solution.py:207
  594.2 1.8 add_convert_fusion.1
  (156 shorter events, 37.1 us)
Async XLA Ops:
  7.2 13.6 %copy-start = (bf16[2,512,1024]{2,1,0:T(8,128)(2,1)S(1)}, bf16[2,512,1024]{2,1,0:T(8,128)(2,1)}, u32[]{:S(2)}) copy-start(bf16[2,512,1024]{2,1,0:T(8,128)(2,1)} %param.16) | copy-start | bytes 6291460
  7.2 88.6 %all-reduce.3.cloned.1.call-start = ((), (), s32[]{:S(2)}) async-start(), calls=%async_computation.5 | async-start | bytes 4194304 | tf_op jit(solution)/shard_map/psum | solution.py:109
  11.8 6.6 %copy-start.13 = (s32[1024]{0:T(1024)}, s32[1024]{0:T(1024)S(1)}, u32[]{:S(2)}) copy-start(s32[1024]{0:T(1024)S(1)} %pad_clamp_fusion.4) | copy-start | bytes 12292
  14.3 8.6 %copy-start.15 = (s32[1024]{0:T(1024)}, s32[1024]{0:T(1024)S(1)}, u32[]{:S(2)}) copy-start(s32[1024]{0:T(1024)S(1)} %pad_clamp_fusion.3) | copy-start | bytes 12292
  20.7 2.2 copy-start.1
  28.2 0.8 copy-start.9
  106.6 97.4 %all-to-all-start = ((bf16[64,16,1024]{2,1,0:T(8,128)(2,1)}), bf16[64,16,1024]{2,1,0:T(8,128)(2,1)}, u32[]{:S(2)}, u32[]{:S(2)}) async-start(bf16[64,16,1024]{2,1,0:T(8,128)(2,1)} %broadcast_select_fusion.1), calls=%async_computation | async-start | bytes 4194304 | tf_op jit(solution)/shard_map/all_to_all | solution.py:112
  117.6 175.2 %all-gather.2.cloned.1.call-start = ((), (), s32[]{:S(2)}) async-start(), calls=%async_computation.6 | async-start | bytes 8519680 | tf_op jit(solution)/shard_map/all_gather | solution.py:139
  203.9 4.7 copy-start.6
  204.0 5.8 copy-start.17
  220.8 144.7 %all-to-all-start.1 = ((s32[64,1,1]{2,1,0:T(1,128)}), s32[64,1,1]{2,1,0:T(1,128)S(1)}, u32[]{:S(2)}, u32[]{:S(2)}) async-start(s32[64,1,1]{2,1,0:T(1,128)} %copy.91), calls=%async_computation.1 | async-start | bytes 65536 | tf_op jit(solution)/shard_map/all_to_all | solution.py:138
  300.4 1.2 copy-start.4
  300.4 1.3 copy-start.10
  302.6 1.3 copy-start.5
  303.9 1.2 copy-start.2
  305.9 1.1 copy-start.3
  310.6 1.2 copy-start.4
  310.7 1.3 copy-start.10
  312.9 1.3 copy-start.5
  314.2 1.2 copy-start.2
  316.2 1.1 copy-start.3
  320.9 1.2 copy-start.4
  320.9 1.3 copy-start.10
  323.1 1.3 copy-start.5
  324.4 1.2 copy-start.2
  326.4 1.1 copy-start.3
  331.2 1.2 copy-start.4
  331.2 1.3 copy-start.10
  333.4 1.3 copy-start.5
  334.7 1.2 copy-start.2
  336.7 1.1 copy-start.3
  365.6 7.6 %copy-start.12 = (bf16[4,128,1,4,64]{1,4,3,2,0:T(8,128)(2,1)S(1)}, bf16[4,128,1,4,64]{1,4,3,2,0:T(8,128)(2,1)}, u32[]{:S(2)}) copy-start(bf16[4,128,1,4,64]{1,4,3,2,0:T(8,128)(2,1)} %get-tuple-element.50) | copy-start | bytes 786436
  365.6 57.2 %all-to-all-start.2 = ((bf16[64,1,128,128]{3,2,1,0:T(8,128)(2,1)}), bf16[64,1,128,128]{3,2,1,0:T(8,128)(2,1)}, u32[]{:S(2)}, u32[]{:S(2)}) async-start(bf16[64,1,128,128]{3,2,1,0:T(8,128)(2,1)} %bitcast.379), calls=%async_computation.2 | async-start | bytes 4194304 | tf_op jit(solution)/shard_map/all_to_all | solution.py:179
  426.8 8.8 %copy-start.7 = (bf16[1024,2,64]{0,2,1:T(8,128)(2,1)S(1)}, bf16[1024,2,64]{0,2,1:T(8,128)(2,1)}, u32[]{:S(2)}) copy-start(bf16[1024,2,64]{0,2,1:T(8,128)(2,1)} %param.18) | copy-start | bytes 786436
  435.6 1.0 copy-start.8
  489.8 59.2 %all-to-all-start.3 = ((bf16[64,16,1024]{2,1,0:T(8,128)(2,1)}), bf16[64,16,1024]{2,1,0:T(8,128)(2,1)}, u32[]{:S(2)}, u32[]{:S(2)}) async-start(bf16[64,16,1024]{2,1,0:T(8,128)(2,1)} %broadcast_select_fusion), calls=%async_computation.3 | async-start | bytes 4194304 | tf_op jit(solution)/shard_map/all_to_all | solution.py:196
  497.8 96.4 %reduce-scatter.2.cloned.1.call-start = ((), (), s32[]{:S(2)}) async-start(), calls=%async_computation.7 | async-start | bytes 2621440 | tf_op jit(solution)/shard_map/reduce_scatter | solution.py:207
  548.9 4.6 copy-start.14
  556.3 5.3 copy-start.16
  566.9 0.9 copy-start.11
Sparse Core Ops, SparseCore 0:
  28.3 67.4 all-reduce.2
  209.9 82.8 all-gather.1
  567.0 27.1 reduce-scatter.1
where the time goes:
time: 614 us; the launch traced here: 603 us
  waiting for transfers between devices  245 us (40%)
  other arithmetic  121 us (20%)
  local copies, waits for them, and re-layouts  103 us (17%)
  blocking collectives  42.7 us (7%)
  matrix products  40.3 us (7%)
  starting transfers between devices  35.6 us (6%)
  between operations  14.6 us (2%)
    gather x6, other arithmetic, unpack_rows(): slot_ids = within - starts[peer_ids]  80.3 us
    psum x1, waiting for transfers between devices, shards(): mlp_sum = lax.psum(partial_mlp, 'head')  66.3 us
    all_gather x1, waiting for transfers between devices, shards(): all_keys = lax.all_gather(key_value_pairs, 'det', axis=0, tiled=True)  55.5 us
    all_to_all x1, waiting for transfers between devices, shards(): lax.all_to_all(outbound_back, 'det', split_axis=0, concat_axis=0, tiled=T...  51.1 us
    all_to_all x1, waiting for transfers between devices, shards(): lax.all_to_all(returned, 'det', split_axis=0, concat_axis=0, tiled=True)  49.4 us
    psum x1, blocking collectives, shards(): back_sum = lax.psum(partial_back, 'head').astype(jnp.bfloat16)  42.7 us
    reduce_scatter x1, waiting for transfers between devices, shards(): lax.psum_scatter(input_part, 'head', scatter_dimension=1, tiled=True)  23.1 us
  transfers between devices with their start and end apart: 7, of which 5 were waited for; matrix products, arithmetic and copies ran while one was open for 30% of the time, Pallas kernels for 0%

commit v1 on v0

--- a/solution.py
+++ b/solution.py
@@ -136,7 +136,9 @@
         .reshape(peer_count, per_pair)
     )
     wanted = lax.all_to_all(requests, "det", split_axis=0, concat_axis=0, tiled=True)
-    all_keys = lax.all_gather(key_value_pairs, "det", axis=0, tiled=True)
+    all_keys = jnp.concatenate(
+        lax.all_to_all(jnp.stack([key_value_pairs] * lax.axis_size("det")), "det", 0, 0), axis=0
+    )
     listed = all_keys.reshape(-1, BLOCK_ROWS, 2 * kv_width)[flat_list]
     listed = listed.reshape(blocks_dev, LISTED_COUNT * BLOCK_ROWS, 2 * kv_width)
     kv_heads = kv_width // HEAD_SIZE

time: 614 us -> 741 us (1.21)
  waiting for transfers between devices: 245 us -> 370 us
  starting transfers between devices: 35.6 us -> 47.7 us
    all_to_all x0 -> x1, waiting for transfers between devices: none -> 179 us  [shards(): lax.all_to_all(jnp.stack([key_value_pairs] * lax.axis_size('det')), 'det'...]
    all_gather x1 -> x0, waiting for transfers between devices: 55.5 us -> none  [shards(): all_keys = lax.all_gather(key_value_pairs, 'det', axis=0, tiled=True)]
    all_to_all x0 -> x1, starting transfers between devices: none -> 10.6 us  [shards(): lax.all_to_all(jnp.stack([key_value_pairs] * lax.axis_size('det')), 'det'...]
    scatter x1, local copies, waits for them, and re-layouts: 10 us -> 0.77 us  [shards(): requests = jnp.zeros((slot_count,), jnp.int32).at[position].set(local_ids...]
  transfers between devices with their start and end apart: 7 -> 7, of which waited for: 5 -> 5; matrix products, arithmetic and copies ran while one was open for 30% -> 23% of each run, Pallas kernels for 0% -> 0%
where the time goes in v1:
time: 741 us; the launch traced here: 733 us
  waiting for transfers between devices  370 us (50%)
  other arithmetic  122 us (16%)
  local copies, waits for them, and re-layouts  98 us (13%)
  starting transfers between devices  47.7 us (6%)
  blocking collectives  40.7 us (5%)
  matrix products  39.7 us (5%)
  between operations  14.8 us (2%)
    all_to_all x1, waiting for transfers between devices, shards(): lax.all_to_all(jnp.stack([key_value_pairs] * lax.axis_size('det')), 'det'...  179 us
    gather x6, other arithmetic, unpack_rows(): slot_ids = within - starts[peer_ids]  80.9 us
    psum x1, waiting for transfers between devices, shards(): mlp_sum = lax.psum(partial_mlp, 'head')  66.3 us
    all_to_all x1, waiting for transfers between devices, shards(): lax.all_to_all(outbound_back, 'det', split_axis=0, concat_axis=0, tiled=T...  51 us
    all_to_all x1, waiting for transfers between devices, shards(): lax.all_to_all(returned, 'det', split_axis=0, concat_axis=0, tiled=True)  49.3 us
    psum x1, blocking collectives, shards(): back_sum = lax.psum(partial_back, 'head').astype(jnp.bfloat16)  40.7 us
    reduce_scatter x1, waiting for transfers between devices, shards(): lax.psum_scatter(input_part, 'head', scatter_dimension=1, tiled=True)  24.1 us
  transfers between devices with their start and end apart: 7, of which 5 were waited for; matrix products, arithmetic and copies ran while one was open for 23% of the time, Pallas kernels for 0%

profile of v1, /device:TPU:1, one launch (start us, length us, event | category | flops | bytes accessed | tf_op | source)
XLA Modules:
  0.0 732.8 jit_solution(1447657452326822961)
XLA Ops:
  7.2 4.6 sort.17
  11.8 2.4 scatter_custom_fusion
  14.3 4.1 gather_fusion
  18.4 2.3 fusion.99
  20.8 2.2 fusion.52
  22.9 5.3 gather_fusion.1
  29.5 66.3 %all-reduce.3.cloned.1.call-done = f32[512,1024]{1,0:T(8,128)} async-done(((f32[512,1024]{1,0:T(8,128)}), f32[512,1024]{1,0:T(8,128)}) %all-reduce.3.cloned.1.call-update) | async-done | bytes 2097168 | tf_op jit(solution)/shard_map/psum | solution.py:109
  95.8 2.2 add_convert_fusion
  98.0 5.4 gather_fusion.2
  103.4 3.2 broadcast_select_fusion.1
  106.6 11.7 %all-to-all-start = ((bf16[64,16,1024]{2,1,0:T(8,128)(2,1)}), bf16[64,16,1024]{2,1,0:T(8,128)(2,1)}, u32[]{:S(2)}, u32[]{:S(2)}) async-start(bf16[64,16,1024]{2,1,0:T(8,128)(2,1)} %broadcast_select_fusion.1), calls=%async_computation | async-start | bytes 4194304 | tf_op jit(solution)/shard_map/all_to_all | solution.py:112
  124.2 4.3 compare_select_fusion.12
  128.9 4.4 compare_select_fusion.6
  133.6 35.7 %select_select_fusion.1 = s32[512]{0:T(512)S(1)} fusion(pred[512]{0:T(512)(128)(4,1)S(1)} %get-tuple-element.224, pred[512]{0:T(512)(128)(4,1)S(1)} %get-tuple-element.223, pred[512]{0:T(512)(128)(4,1)S(1)} %get-tuple-element.222, pred[512]{0:T(512)(128)(4,1)S(1)} %get-tuple-element.221, pred[512]{0:T(512)(128)(4,1)S(1)} %get-tuple-element.220, ...), kind=kLoop, calls=%fused_computation.250 | loop fusion | flops 29184 | bytes 33508 | tf_op jit(solution)/shard_map/gather | solution.py:33
  169.4 35.7 %select_select_fusion = s32[512]{0:T(512)S(1)} fusion(pred[512]{0:T(512)(128)(4,1)S(1)} %get-tuple-element.167, pred[512]{0:T(512)(128)(4,1)S(1)} %get-tuple-element.166, pred[512]{0:T(512)(128)(4,1)S(1)} %get-tuple-element.165, pred[512]{0:T(512)(128)(4,1)S(1)} %get-tuple-element.164, pred[512]{0:T(512)(128)(4,1)S(1)} %get-tuple-element.163, ...), kind=kLoop, calls=%fused_computation.249 | loop fusion | flops 29184 | bytes 33508 | tf_op jit(solution)/shard_map/gather | solution.py:33
  205.7 4.6 gather_fusion.3
  210.8 5.2 stack.2
  216.1 10.6 %all-to-all-start.1 = ((bf16[64,512,128]{2,1,0:T(8,128)(2,1)}), bf16[64,512,128]{2,1,0:T(8,128)(2,1)}, u32[]{:S(2)}, u32[]{:S(2)}) async-start(bf16[64,512,128]{2,1,0:T(8,128)(2,1)} %stack.2), calls=%async_computation.1 | async-start | bytes 16777216 | tf_op jit(solution)/shard_map/all_to_all | solution.py:140
  227.9 1.9 copy.88
  231.6 1.5 convolution_convert_fusion
  233.6 178.9 %all-to-all-done.1 = bf16[64,512,128]{2,1,0:T(8,128)(2,1)} async-done(((bf16[64,512,128]{2,1,0:T(8,128)(2,1)}), bf16[64,512,128]{2,1,0:T(8,128)(2,1)}, u32[]{:S(2)}, u32[]{:S(2)}) %all-to-all-start.1) | async-done | bytes 8388640 | tf_op jit(solution)/shard_map/all_to_all | solution.py:140
  412.4 6.1 all-to-all-start.2
  418.5 5.6 gather_fusion.4
  424.1 41.0 %while.16 = (s32[]{:T(128)}, bf16[4,128,1,4,64]{1,4,3,2,0:T(8,128)(2,1)}, bf16[4,128,1,4,64]{1,4,3,2,0:T(8,128)(2,1)}, bf16[4,2048,1,64]{1,3,2,0:T(8,128)(2,1)},...) while((s32[]{:T(128)}, ...), condition=%wide.region_10.11_spmd, body=%wide.region_6.10_spmd.sunk | while | flops 830700032 | bytes 62289140 | solution.py:162
  428.4 1.3 fusion.137
  429.7 1.1 fusion.138
  431.7 1.1 fusion.139
  432.8 1.6 fusion.136
  438.7 1.3 fusion.137
  440.0 1.1 fusion.138
  442.0 1.1 fusion.139
  443.1 1.6 fusion.136
  448.9 1.3 fusion.137
  452.2 1.1 fusion.139
  453.3 1.6 fusion.136
  459.2 1.3 fusion.137
  462.5 1.1 fusion.139
  463.6 1.6 fusion.136
  465.2 2.0 copy.93
  467.2 1.5 concatenate.10
  468.7 2.0 copy.92
  470.7 1.5 concatenate.9
  472.2 3.1 pad_maximum_fusion
  475.3 4.2 copy.94
  479.5 1.9 broadcast_in_dim.43
  481.4 10.0 %scatter_fusion = bf16[64,128,128]{2,1,0:T(8,128)(2,1)} fusion(bf16[64,128,128]{2,1,0:T(8,128)(2,1)} %broadcast_in_dim.43, s32[64]{0:T(128)S(1)} %get-tuple-element.385, bf16[64,128,128]{2,1,0:T(8,128)(2,1)} %copy.94), kind=kCustom, calls=%fused_computation.11 | custom fusion | bytes 6291712 | tf_op jit(solution)/shard_map/scatter | solution.py:178
  491.4 11.0 %all-to-all-start.3 = ((bf16[64,1,128,128]{3,2,1,0:T(8,128)(2,1)}), bf16[64,1,128,128]{3,2,1,0:T(8,128)(2,1)}, u32[]{:S(2)}, u32[]{:S(2)}) async-start(bf16[64,1,128,128]{3,2,1,0:T(8,128)(2,1)} %bitcast.379), calls=%async_computation.3 | async-start | bytes 4194304 | tf_op jit(solution)/shard_map/all_to_all | solution.py:181
  502.6 1.2 reduce.62
  504.1 49.3 %all-to-all-done.3 = bf16[64,1,128,128]{3,2,1,0:T(8,128)(2,1)} async-done(((bf16[64,1,128,128]{3,2,1,0:T(8,128)(2,1)}), bf16[64,1,128,128]{3,2,1,0:T(8,128)(2,1)}, u32[]{:S(2)}, u32[]{:S(2)}) %all-to-all-start.3) | async-done | bytes 2097184 | tf_op jit(solution)/shard_map/all_to_all | solution.py:181
  553.3 4.0 bitcast_convert_fusion
  557.4 8.8 %scatter_fusion.1 = f32[4,128,128]{2,1,0:T(8,128)S(1)} fusion(f32[4,128,128]{2,1,0:T(8,128)S(1)} %broadcast_in_dim.42, s32[64]{0:T(128)S(1)} %fusion.73, f32[64,128,128]{2,1,0:T(8,128)} %bitcast_convert_fusion), kind=kCustom, calls=%fused_computation.12 | custom fusion | flops 1048576 | bytes 12583168 | tf_op jit(solution)/shard_map/scatter-add | solution.py:186
  567.2 1.8 convolution_add_fusion
  569.1 40.7 %all-reduce.4 = bf16[512,1024]{1,0:T(8,128)(2,1)S(1)} all-reduce(f32[512,1024]{1,0:T(8,128)} %convolution_add_fusion), channel_id=1, replica_groups=mesh['det'=64,'head'=4] {'head'}, use_global_device_ids=true, to_apply=%region_15.16 | all-reduce | flops 524288 | bytes 3145728 | tf_op jit(solution)/shard_map/psum | solution.py:196
  609.8 5.4 gather_fusion.5
  615.2 3.2 broadcast_select_fusion
  618.3 8.3 %all-to-all-start.4 = ((bf16[64,16,1024]{2,1,0:T(8,128)(2,1)}), bf16[64,16,1024]{2,1,0:T(8,128)(2,1)}, u32[]{:S(2)}, u32[]{:S(2)}) async-start(bf16[64,16,1024]{2,1,0:T(8,128)(2,1)} %broadcast_select_fusion), calls=%async_computation.4 | async-start | bytes 4194304 | tf_op jit(solution)/shard_map/all_to_all | solution.py:198
  626.7 51.0 %all-to-all-done.4 = bf16[64,16,1024]{2,1,0:T(8,128)(2,1)} async-done(((bf16[64,16,1024]{2,1,0:T(8,128)(2,1)}), bf16[64,16,1024]{2,1,0:T(8,128)(2,1)}, u32[]{:S(2)}, u32[]{:S(2)}) %all-to-all-start.4) | async-done | bytes 2097184 | tf_op jit(solution)/shard_map/all_to_all | solution.py:198
  677.7 4.6 gather_fusion.6
  682.3 2.8 gather_fusion.7
  685.1 5.3 fusion.53
  690.4 5.2 gather_fusion.8
  697.7 2.2 reshape.1339
  699.8 24.1 %reduce-scatter.2.cloned.1.call-done = f32[512,256]{1,0:T(8,128)} async-done(((f32[512,1024]{1,0:T(8,128)}), f32[512,256]{1,0:T(8,128)}) %reduce-scatter.2.cloned.1.call-update) | async-done | bytes 524304 | tf_op jit(solution)/shard_map/reduce_scatter | solution.py:209
  723.9 1.8 add_convert_fusion.1
  (160 shorter events, 38.7 us)
Async XLA Ops:
  7.2 13.6 %copy-start = (bf16[2,512,1024]{2,1,0:T(8,128)(2,1)S(1)}, bf16[2,512,1024]{2,1,0:T(8,128)(2,1)}, u32[]{:S(2)}) copy-start(bf16[2,512,1024]{2,1,0:T(8,128)(2,1)} %param.16) | copy-start | bytes 6291460
  7.2 88.6 %all-reduce.3.cloned.1.call-start = ((), (), s32[]{:S(2)}) async-start(), calls=%async_computation.6 | async-start | bytes 4194304 | tf_op jit(solution)/shard_map/psum | solution.py:109
  11.8 6.6 copy-start.14
  14.3 8.6 %copy-start.16 = (s32[1024]{0:T(1024)}, s32[1024]{0:T(1024)S(1)}, u32[]{:S(2)}) copy-start(s32[1024]{0:T(1024)S(1)} %pad_clamp_fusion.3) | copy-start | bytes 12292
  20.7 2.2 copy-start.1
  28.2 0.8 copy-start.9
  106.6 99.2 %all-to-all-start = ((bf16[64,16,1024]{2,1,0:T(8,128)(2,1)}), bf16[64,16,1024]{2,1,0:T(8,128)(2,1)}, u32[]{:S(2)}, u32[]{:S(2)}) async-start(bf16[64,16,1024]{2,1,0:T(8,128)(2,1)} %broadcast_select_fusion.1), calls=%async_computation | async-start | bytes 4194304 | tf_op jit(solution)/shard_map/all_to_all | solution.py:112
  205.7 4.7 copy-start.6
  216.1 10.7 %copy-start.18 = (s32[4,16]{1,0:T(4,128)S(1)}, s32[4,16]{1,0:T(4,128)}, u32[]{:S(2)}) copy-start(s32[4,16]{1,0:T(4,128)} %param.14) | copy-start | bytes 772
  216.1 10.8 %copy-start.10 = (bf16[512,256]{1,0:T(8,128)(2,1)S(1)}, bf16[512,256]{1,0:T(8,128)(2,1)}, u32[]{:S(2)}) copy-start(bf16[512,256]{1,0:T(8,128)(2,1)} %param.19) | copy-start | bytes 786436
  216.1 196.4 %all-to-all-start.1 = ((bf16[64,512,128]{2,1,0:T(8,128)(2,1)}), bf16[64,512,128]{2,1,0:T(8,128)(2,1)}, u32[]{:S(2)}, u32[]{:S(2)}) async-start(bf16[64,512,128]{2,1,0:T(8,128)(2,1)} %stack.2), calls=%async_computation.1 | async-start | bytes 16777216 | tf_op jit(solution)/shard_map/all_to_all | solution.py:140
  412.4 78.9 %all-to-all-start.2 = ((s32[64,1,1]{2,1,0:T(1,128)}), s32[64,1,1]{2,1,0:T(1,128)S(1)}, u32[]{:S(2)}, u32[]{:S(2)}) async-start(s32[64,1,1]{2,1,0:T(1,128)} %copy.91), calls=%async_computation.2 | async-start | bytes 65536 | tf_op jit(solution)/shard_map/all_to_all | solution.py:138
  426.2 1.2 copy-start.4
  426.2 1.3 copy-start.11
  428.4 1.3 copy-start.5
  429.7 1.2 copy-start.2
  431.7 1.1 copy-start.3
  436.4 1.2 copy-start.4
  436.4 1.3 copy-start.11
  438.7 1.3 copy-start.5
  440.0 1.2 copy-start.2
  442.0 1.1 copy-start.3
  446.7 1.2 copy-start.4
  446.7 1.3 copy-start.11
  448.9 1.3 copy-start.5
  450.2 1.2 copy-start.2
  452.2 1.1 copy-start.3
  456.9 1.2 copy-start.4
  457.0 1.3 copy-start.11
  459.2 1.3 copy-start.5
  460.5 1.2 copy-start.2
  462.5 1.1 copy-start.3
  491.4 12.5 %copy-start.13 = (bf16[4,128,1,4,64]{1,4,3,2,0:T(8,128)(2,1)S(1)}, bf16[4,128,1,4,64]{1,4,3,2,0:T(8,128)(2,1)}, u32[]{:S(2)}) copy-start(bf16[4,128,1,4,64]{1,4,3,2,0:T(8,128)(2,1)} %get-tuple-element.50) | copy-start | bytes 786436
  491.4 62.0 %all-to-all-start.3 = ((bf16[64,1,128,128]{3,2,1,0:T(8,128)(2,1)}), bf16[64,1,128,128]{3,2,1,0:T(8,128)(2,1)}, u32[]{:S(2)}, u32[]{:S(2)}) async-start(bf16[64,1,128,128]{3,2,1,0:T(8,128)(2,1)} %bitcast.379), calls=%async_computation.3 | async-start | bytes 4194304 | tf_op jit(solution)/shard_map/all_to_all | solution.py:181
  557.4 8.8 %copy-start.7 = (bf16[1024,2,64]{0,2,1:T(8,128)(2,1)S(1)}, bf16[1024,2,64]{0,2,1:T(8,128)(2,1)}, u32[]{:S(2)}) copy-start(bf16[1024,2,64]{0,2,1:T(8,128)(2,1)} %param.18) | copy-start | bytes 786436
  566.2 1.0 copy-start.8
  618.3 8.3 %copy-start.19 = (s32[512,1]{0,1:T(1,128)S(1)}, s32[512,1]{0,1:T(1,128)}, u32[]{:S(2)}) copy-start(s32[512,1]{0,1:T(1,128)} %get-tuple-element.387) | copy-start | bytes 6148
  618.3 59.4 %all-to-all-start.4 = ((bf16[64,16,1024]{2,1,0:T(8,128)(2,1)}), bf16[64,16,1024]{2,1,0:T(8,128)(2,1)}, u32[]{:S(2)}, u32[]{:S(2)}) async-start(bf16[64,16,1024]{2,1,0:T(8,128)(2,1)} %broadcast_select_fusion), calls=%async_computation.4 | async-start | bytes 4194304 | tf_op jit(solution)/shard_map/all_to_all | solution.py:198
  626.6 97.3 %reduce-scatter.2.cloned.1.call-start = ((), (), s32[]{:S(2)}) async-start(), calls=%async_computation.7 | async-start | bytes 2621440 | tf_op jit(solution)/shard_map/reduce_scatter | solution.py:209
  677.7 4.6 copy-start.15
  685.1 5.3 copy-start.17
  695.6 0.9 copy-start.12
Sparse Core Ops, SparseCore 0:
  28.3 67.4 all-reduce.2
  695.8 28.0 reduce-scatter.1
